TPU v7x, 32 devices: a whole 2x2x4 slice. The times are simulated.
32 devices in a mesh: tile: 4 (over z), chan: 4 (over y, x), tm: 2 (over core).
Axes of the slice: x: 2, y: 2, z: 4, core: 2. Of those that a mesh axis runs over, the one named last changes fastest.
Arguments:
- observed_values: bfloat16 [2, 65536, 128], P('tm', ('tile', 'chan')), may hold values from -6 to 6
- observed_tile: int32 [2, 65536, 1], P('tm', ('tile', 'chan')), may hold values from 0 to 3; in each aligned block of 4096 rows (0 to 4095, 4096 to 8191, ..., all dimensions but the last counted through in order) at most 2048 rows name the same one
- observed_cell: int32 [2, 65536], P('tm', ('tile', 'chan')), may hold values from 0 to 2047
- patch_weight: bfloat16 [4, 256, 256], P(None, None, 'chan'), may hold values from -0.1875 to 0.1875
- depth_weight: bfloat16 [9, 256], P(None, 'chan'), may hold values from -2 to 2
- owners: int32 [4, 4], replicated, may hold values from 0 to 3, as said below
Outputs:
- owned: bfloat16 [4, 2, 4, 64, 256], P('tile', 'tm', None, None, 'chan')
Inputs may be any that keep to these rules, and one draw needn't show every extreme that they name: `observed_tile`: in the rows of one device at most 2048 name the same tile. owners[t, j] - t is the same modulo 4 for every t and differs between any two j, so every row and every column of owners is a permutation.
All inputs are finite; a program needn't handle non-finite values.
Results may differ from a plain program's by a relative error of at most 0.014.
Values may be sent and summed in bfloat16 or wider, within the bound.
A program may use at most 64 MiB of HBM per device.

v0:
```python
import jax
import jax.numpy as jnp
from jax import lax
from jax.sharding import PartitionSpec as P

V = 128
HS = 32
WS = 64


def padded(x, sides, width):
    for axis, dim in sides:
        devices, length = (lax.axis_size(axis), x.shape[dim])
        up = [(i, (i + 1) % devices) for i in range(devices - 1)]
        down = [(j, i) for i, j in up]
        last = lax.slice_in_dim(x, length - width, length, axis=dim)
        first = lax.slice_in_dim(x, 0, width, axis=dim)
        before = lax.ppermute(last, axis, up)
        after = lax.ppermute(first, axis, down)
        x = jnp.concatenate([before, x, after], axis=dim)
    return x


def pack_rows(values, destination, placed, tile_count, capacity):
    match = (destination[:, None] == lax.iota(jnp.int32, tile_count)[None, :]).astype(jnp.int32)
    earlier = jnp.cumsum(match, axis=0) - match
    position = jnp.sum(earlier * match, axis=1)
    slot_index = destination * capacity + position
    width = values.shape[1]
    sent_values = jnp.zeros((tile_count * capacity, width), jnp.bfloat16).at[slot_index].set(values)
    sent_cells = jnp.full((tile_count * capacity,), -1, jnp.int32).at[slot_index].set(placed)
    return (
        sent_values.reshape(tile_count, capacity, width),
        sent_cells.reshape(tile_count, capacity),
    )


def grid_block(arrived_values, arrived_cells, first_cell):
    cell_ids = first_cell + lax.iota(jnp.int32, 128)
    matches = cell_ids[:, None] == arrived_cells[None, :]
    totals = jnp.dot(
        matches.astype(jnp.bfloat16), arrived_values, preferred_element_type=jnp.float32
    )
    counts = jnp.sum(matches.astype(jnp.float32), axis=1)
    return (totals, counts)


def patch_rows(field, weight, row_start, row_count):
    slab = lax.dynamic_slice_in_dim(field, 2 * row_start, 2 * row_count, 0)
    depth_in = field.shape[2]
    result = jnp.zeros((row_count * (field.shape[1] // 2), weight.shape[2]), jnp.float32)
    for tap_row in range(2):
        for tap_col in range(2):
            window = slab[tap_row::2, tap_col::2, :].reshape(-1, depth_in)
            result = result + jnp.dot(
                window, weight[tap_row * 2 + tap_col], preferred_element_type=jnp.float32
            )
    return result.reshape(row_count, field.shape[1] // 2, weight.shape[2])


def local(observed_values, observed_tile, observed_cell, patch_weight, depth_weight, owners):
    tile_count = lax.axis_size("tile")
    slot_count = lax.axis_size("tm")
    values = observed_values[0]
    capacity = 2 * values.shape[0] // tile_count
    sent_values, sent_cells = pack_rows(
        values, observed_tile[0, :, 0], observed_cell[0], tile_count, capacity
    )
    arrived = (
        lax.all_to_all(sent_values, "tile", split_axis=0, concat_axis=0, tiled=True),
        lax.all_to_all(sent_cells, "tile", split_axis=0, concat_axis=0, tiled=True),
    )
    arrived_values = arrived[0].reshape(-1, V)
    arrived_cells = arrived[1].reshape(-1)
    cell_count = HS * WS
    firsts = jnp.arange(cell_count // 128, dtype=jnp.int32) * 128
    totals, counts = lax.map(
        lambda first_cell: grid_block(arrived_values, arrived_cells, first_cell), firsts
    )
    totals = totals.reshape(cell_count, V)
    counts = counts.reshape(cell_count)
    totals, counts = (
        lax.psum(totals.astype(jnp.bfloat16), "chan").astype(jnp.float32),
        lax.psum(counts.astype(jnp.bfloat16), "chan").astype(jnp.float32),
    )
    means = (totals / jnp.maximum(counts, 1.0)[:, None]).astype(jnp.bfloat16)
    means = means.reshape(HS, WS, V)
    out_rows = HS // (2 * slot_count)
    half_cols = WS // 2
    stacked = lax.all_gather(means, "tm", axis=2, tiled=True)
    encoded = patch_rows(stacked, patch_weight, lax.axis_index("tm") * out_rows, out_rows)
    hidden = jax.nn.gelu(encoded).astype(jnp.bfloat16)
    rimmed = padded(hidden, ((("tile", "tm"), 0),), 2)
    widened = jnp.pad(rimmed, ((0, 0), (2, 2), (0, 0))).astype(jnp.float32)
    depth = jnp.zeros(hidden.shape, jnp.float32)
    for tap_row in range(3):
        for tap_col in range(3):
            shifted = widened[
                2 * tap_row : 2 * tap_row + out_rows, 2 * tap_col : 2 * tap_col + half_cols, :
            ]
            depth = depth + shifted * depth_weight[tap_row * 3 + tap_col].astype(jnp.float32)
    latent = (hidden.astype(jnp.float32) + depth).astype(jnp.bfloat16)
    channels = latent.shape[2]
    pieces = latent.reshape(tile_count, -1, channels)
    own_row = lax.dynamic_index_in_dim(owners, lax.axis_index("tile"), 0, keepdims=False)
    order = lax.iota(jnp.int32, tile_count)
    chosen = jnp.sum(
        order[None, :] * (own_row[None, :] == order[:, None]).astype(jnp.int32), axis=1
    )
    outgoing = pieces[chosen]
    received = lax.all_to_all(outgoing, "tile", split_axis=0, concat_axis=0, tiled=True)
    return received.reshape(1, 1, tile_count, -1, channels)


def solution(mesh):
    placed = (
        P("tm", ("tile", "chan"), None),
        P("tm", ("tile", "chan"), None),
        P("tm", ("tile", "chan")),
        P(None, None, "chan"),
        P(None, "chan"),
        P(),
    )
    return jax.shard_map(
        local,
        mesh=mesh,
        in_specs=placed,
        out_specs=P("tile", "tm", None, None, "chan"),
        check_vma=False,
    )
```

profile of v0, /device:TPU:0, one launch (start us, length us, event | category | flops | bytes accessed | tf_op | source)
XLA Modules:
  0.0 239.9 jit_solution(12376599636071230112)
XLA Ops:
  10.6 16.3 %scatter_custom_fusion = s32[8192]{0:T(1024)} fusion(s32[4096]{0:T(1024)S(1)} %bitcast.137, s32[4096]{0:T(1024)} %bitcast.141, s32[]{:T(128)} %constant.27.clone.1), kind=kCustom, calls=%fused_computation.77 | custom fusion | bytes 33280 | tf_op jit(solution)/shard_map/scatter | solution.py:31
  26.9 6.3 %all-to-all-start = ((s32[4,1,2048]{2,1,0:T(1,128)}), s32[4,1,2048]{2,1,0:T(1,128)S(1)}, u32[]{:S(2)}, u32[]{:S(2)}) async-start(s32[4,1,2048]{2,1,0:T(1,128)} %bitcast.10), calls=%async_computation | async-start | bytes 65536 | tf_op jit(solution)/shard_map/all_to_all | solution.py:71
  33.2 12.4 %scatter_custom_fusion.1 = bf16[8192,128]{1,0:T(8,128)(2,1)} fusion(s32[4096]{0:T(1024)S(1)} %bitcast.138, bf16[1,4096,128]{2,1,0:T(8,128)(2,1)S(1)} %copy-done, bf16[]{:T(256)} %constant.19.clone.1), kind=kCustom, calls=%fused_computation.15 | custom fusion | bytes 3145730 | tf_op jit(solution)/shard_map/scatter | solution.py:30
  45.6 5.1 %all-to-all-start.1 = ((bf16[4,2048,128]{2,1,0:T(8,128)(2,1)}), bf16[4,2048,128]{2,1,0:T(8,128)(2,1)S(1)}, u32[]{:S(2)}, u32[]{:S(2)}) async-start(bf16[4,2048,128]{2,1,0:T(8,128)(2,1)} %bitcast.12), calls=%async_computation.1 | async-start | bytes 4194304 | tf_op jit(solution)/shard_map/all_to_all | solution.py:70
  50.8 47.6 %all-to-all-done.1 = bf16[4,2048,128]{2,1,0:T(8,128)(2,1)S(1)} async-done(((bf16[4,2048,128]{2,1,0:T(8,128)(2,1)}), bf16[4,2048,128]{2,1,0:T(8,128)(2,1)S(1)}, u32[]{:S(2)}, u32[]{:S(2)}) %all-to-all-start.1) | async-done | bytes 2097184 | tf_op jit(solution)/shard_map/all_to_all | solution.py:70
  98.4 56.3 %while.12 = (s32[]{:T(128)}, bf16[16,128,128]{2,1,0:T(8,128)(2,1)}, bf16[16,128]{1,0:T(8,128)(2,1)S(1)}, s32[16]{0:T(128)S(1)}, s32[4,2048]{1,0:T(4,128)S(1)}, /...) while((s32[]{:T(128)}, bf16[16,128,128]{2,1,0:T(8,128)(2,1)}, bf16[16,128]{1,0:T(8,128)(2,1)S(1)}, ...), condition=%wide.region_7.8_spmd, body=%wide.region_5.7_spmd.sunk | while | flops 272629760 | bytes 2296681 | solution.py:77
  99.7 1.5 fusion.67
  103.3 1.5 fusion.67
  106.8 1.5 fusion.67
  117.3 1.5 fusion.67
  120.9 1.5 fusion.67
  124.4 1.5 fusion.67
  131.4 1.5 fusion.67
  134.9 1.5 fusion.67
  138.5 1.5 fusion.67
  145.5 1.5 fusion.67
  152.5 1.5 fusion.67
  154.8 10.1 %psum.15 = bf16[2048]{0:T(1024)(128)(2,1)S(1)} all-reduce(bf16[2048]{0:T(1024)(128)(2,1)S(1)} %bitcast.140), channel_id=1, replica_groups=mesh['tile'=4,'chan'=4,'tm'=2] {'chan'}, use_global_device_ids=true, to_apply=%region_9.10 | all-reduce | flops 2048 | bytes 8192 | tf_op jit(solution)/shard_map/psum | solution.py:84
  164.9 34.5 %all-reduce.3.cloned.1.call-done = bf16[2048,128]{1,0:T(8,128)(2,1)} async-done(((bf16[2048,128]{1,0:T(8,128)(2,1)}), bf16[2048,128]{1,0:T(8,128)(2,1)}) %all-reduce.3.cloned.1.call-update) | async-done | bytes 524304 | tf_op jit(solution)/shard_map/psum | solution.py:83
  199.4 2.2 divide_convert_fusion
  202.5 8.1 %all-gather.2.cloned.1.call-done = bf16[32,64,256]{2,1,0:T(8,128)(2,1)} async-done(((bf16[32,64,128]{2,1,0:T(8,128)(2,1)}), bf16[32,64,256]{2,1,0:T(8,128)(2,1)}) %all-gather.2.cloned.1.call-update) | async-done | bytes 1048592 | tf_op jit(solution)/shard_map/all_gather | solution.py:90
  214.1 2.2 collective-permute-start
  217.6 2.9 %collective-permute-done.1 = bf16[2,32,64]{2,1,0:T(8,128)(2,1)S(1)} collective-permute-done((bf16[2,32,64]{2,1,0:T(8,128)(2,1)S(1)}, bf16[2,32,64]{2,1,0:T(8,128)(2,1)S(1)}, u32[]{:S(2)}, u32[]{:S(2)}) %collective-permute-start.1) | collective-permute-done | bytes 8224 | tf_op jit(solution)/shard_map/ppermute | solution.py:19
  221.4 11.0 %all_to_all.22 = bf16[4,2,2048]{2,1,0:T(2,128)(2,1)S(1)} all-to-all(bf16[4,2,2048]{2,1,0:T(2,128)(2,1)S(1)} %reshape.214), channel_id=1, replica_groups=mesh['tile'=4,'chan'=4,'tm'=2] {'tile'}, dimensions={0} | all-to-all | bytes 65536 | tf_op jit(solution)/shard_map/all_to_all | solution.py:111
  (132 shorter events, 51.0 us)
Async XLA Ops:
  6.5 26.7 %copy-start = (bf16[1,4096,128]{2,1,0:T(8,128)(2,1)S(1)}, bf16[1,4096,128]{2,1,0:T(8,128)(2,1)}, u32[]{:S(2)}) copy-start(bf16[1,4096,128]{2,1,0:T(8,128)(2,1)} %param.8) | copy-start | bytes 3145732
  26.9 18.8 %all-to-all-start = ((s32[4,1,2048]{2,1,0:T(1,128)}), s32[4,1,2048]{2,1,0:T(1,128)S(1)}, u32[]{:S(2)}, u32[]{:S(2)}) async-start(s32[4,1,2048]{2,1,0:T(1,128)} %bitcast.10), calls=%async_computation | async-start | bytes 65536 | tf_op jit(solution)/shard_map/all_to_all | solution.py:71
  45.6 52.7 %all-to-all-start.1 = ((bf16[4,2048,128]{2,1,0:T(8,128)(2,1)}), bf16[4,2048,128]{2,1,0:T(8,128)(2,1)S(1)}, u32[]{:S(2)}, u32[]{:S(2)}) async-start(bf16[4,2048,128]{2,1,0:T(8,128)(2,1)} %bitcast.12), calls=%async_computation.1 | async-start | bytes 4194304 | tf_op jit(solution)/shard_map/all_to_all | solution.py:70
  50.7 148.7 %all-reduce.3.cloned.1.call-start = ((), (), s32[]{:S(2)}) async-start(), calls=%async_computation.3 | async-start | bytes 1048576 | tf_op jit(solution)/shard_map/psum | solution.py:83
  154.7 47.8 %copy-start.2 = (bf16[9,64]{1,0:T(8,128)(2,1)S(1)}, bf16[9,64]{1,0:T(8,128)(2,1)}, u32[]{:S(2)}) copy-start(bf16[9,64]{1,0:T(8,128)(2,1)} %param.12) | copy-start | bytes 3460
  154.7 58.4 %copy-start.1 = (bf16[4,256,64]{1,2,0:T(8,128)(2,1)S(1)}, bf16[4,256,64]{1,2,0:T(8,128)(2,1)}, u32[]{:S(2)}) copy-start(bf16[4,256,64]{1,2,0:T(8,128)(2,1)} %param.11) | copy-start | bytes 393220
  154.7 55.8 %all-gather.2.cloned.1.call-start = ((), (), s32[]{:S(2)}) async-start(), calls=%async_computation.4 | async-start | bytes 1572864 | tf_op jit(solution)/shard_map/all_gather | solution.py:90
  214.1 3.5 %collective-permute-start = (bf16[2,32,64]{2,1,0:T(8,128)(2,1)S(1)}, bf16[2,32,64]{2,1,0:T(8,128)(2,1)S(1)}, u32[]{:S(2)}, u32[]{:S(2)}) collective-permute-start(bf16[2,32,64]{2,1,0:T(8,128)(2,1)S(1)} %get-tuple-element.52), channel_id=1, source_target_pairs={{0,1},{1,8},{8,9},{9,16},{16,17},{17,24},{24,25},{2,3},{3,10},{10,... | collective-permute-start | bytes 24584 | tf_op jit(solution)/shard_map/ppermute | solution.py:18
  216.2 4.2 %collective-permute-start.1 = (bf16[2,32,64]{2,1,0:T(8,128)(2,1)S(1)}, bf16[2,32,64]{2,1,0:T(8,128)(2,1)S(1)}, u32[]{:S(2)}, u32[]{:S(2)}) collective-permute-start(bf16[2,32,64]{2,1,0:T(8,128)(2,1)S(1)} %get-tuple-element.53), channel_id=1, source_target_pairs={{1,0},{8,1},{9,8},{16,9},{17,16},{24,17},{25,24},{3,2},{10,3},{11,... | collective-permute-start | bytes 24584 | tf_op jit(solution)/shard_map/ppermute | solution.py:19
Sparse Core Ops, SparseCore 0:
  154.9 44.5 all-reduce.2
  201.8 8.7 all-gather.1
where the time goes:
time: 241 us; the launch traced here: 240 us
  waiting for transfers between devices  93.1 us (39%)
  local copies, waits for them, and re-layouts  45 us (19%)
  other arithmetic  27.5 us (11%)
  matrix products  24.4 us (10%)
  blocking collectives  21.1 us (9%)
  starting transfers between devices  14.9 us (6%)
  between operations  13.6 us (6%)
    all_to_all x1, waiting for transfers between devices, local(): lax.all_to_all(sent_values, 'tile', split_axis=0, concat_axis=0, tiled=True)  47.6 us
    psum x1, waiting for transfers between devices, local(): lax.psum(totals.astype(jnp.bfloat16), 'chan').astype(jnp.float32)  34.5 us
    dot_general x16, matrix products, grid_block(): jnp.dot(matches.astype(jnp.bfloat16), arrived_values, preferred_element_t...  23.7 us
    scatter x1, local copies, waits for them, and re-layouts, pack_rows(): jnp.full((tile_count * capacity,), -1, jnp.int32).at[slot_index].set(placed)  16.3 us
    scatter x1, local copies, waits for them, and re-layouts, pack_rows(): jnp.zeros((tile_count * capacity, width), jnp.bfloat16).at[slot_index]  12.4 us
    add x16, other arithmetic, grid_block(): cell_ids = first_cell + lax.iota(jnp.int32, 128)  11 us
    all_to_all x1, blocking collectives, local(): lax.all_to_all(outgoing, 'tile', split_axis=0, concat_axis=0, tiled=True)  11 us
    dynamic_slice x16, local copies, waits for them, and re-layouts, local(): lax.map(lambda first_cell: grid_block(arrived_values, arrived_cells, firs...  10.7 us
  transfers between devices with their start and end apart: 6, of which 4 were waited for; matrix products, arithmetic and copies ran while one was open for 6% of the time, Pallas kernels for 0%

commit v1 on v0

--- a/solution.py
+++ b/solution.py
@@ -80,7 +80,7 @@
     totals = totals.reshape(cell_count, V)
     counts = counts.reshape(cell_count)
     totals, counts = (
-        lax.psum(totals.astype(jnp.bfloat16), "chan").astype(jnp.float32),
+        jnp.sum(jax.lax.all_gather(totals.astype(jnp.bfloat16), "chan"), 0).astype(jnp.float32),
         lax.psum(counts.astype(jnp.bfloat16), "chan").astype(jnp.float32),
     )
     means = (totals / jnp.maximum(counts, 1.0)[:, None]).astype(jnp.bfloat16)

time: 241 us -> 232 us (0.963)
  waiting for transfers between devices: 93.1 us -> 82.9 us
    psum x1 -> x0, waiting for transfers between devices: 34.5 us -> none  [local(): lax.psum(totals.astype(jnp.bfloat16), 'chan').astype(jnp.float32)]
    all_gather x0 -> x1, waiting for transfers between devices: none -> 24.3 us  [local(): jax.lax.all_gather(totals.astype(jnp.bfloat16), 'chan')]
where the time goes in v1:
time: 232 us; the launch traced here: 231 us
  waiting for transfers between devices  82.9 us (36%)
  local copies, waits for them, and re-layouts  45 us (19%)
  other arithmetic  28.6 us (12%)
  matrix products  24.4 us (11%)
  blocking collectives  21 us (9%)
  starting transfers between devices  14.9 us (6%)
  between operations  13.6 us (6%)
    all_to_all x1, waiting for transfers between devices, local(): lax.all_to_all(sent_values, 'tile', split_axis=0, concat_axis=0, tiled=True)  47.6 us
    all_gather x1, waiting for transfers between devices, local(): jax.lax.all_gather(totals.astype(jnp.bfloat16), 'chan')  24.3 us
    dot_general x16, matrix products, grid_block(): jnp.dot(matches.astype(jnp.bfloat16), arrived_values, preferred_element_t...  23.7 us
    scatter x1, local copies, waits for them, and re-layouts, pack_rows(): jnp.full((tile_count * capacity,), -1, jnp.int32).at[slot_index].set(placed)  16.3 us
    scatter x1, local copies, waits for them, and re-layouts, pack_rows(): jnp.zeros((tile_count * capacity, width), jnp.bfloat16).at[slot_index]  12.4 us
    add x16, other arithmetic, grid_block(): cell_ids = first_cell + lax.iota(jnp.int32, 128)  11 us
    all_to_all x1, blocking collectives, local(): lax.all_to_all(outgoing, 'tile', split_axis=0, concat_axis=0, tiled=True)  11 us
    dynamic_slice x16, local copies, waits for them, and re-layouts, local(): lax.map(lambda first_cell: grid_block(arrived_values, arrived_cells, firs...  10.7 us
  transfers between devices with their start and end apart: 6, of which 4 were waited for; matrix products, arithmetic and copies ran while one was open for 6% of the time, Pallas kernels for 0%

profile of v1, /device:TPU:0, one launch (start us, length us, event | category | flops | bytes accessed | tf_op | source)
XLA Modules:
  0.0 230.8 jit_solution(5552834944763612105)
XLA Ops:
  10.6 16.3 %scatter_custom_fusion = s32[8192]{0:T(1024)} fusion(s32[4096]{0:T(1024)S(1)} %bitcast.138, s32[4096]{0:T(1024)} %bitcast.142, s32[]{:T(128)} %constant.27.clone.1), kind=kCustom, calls=%fused_computation.78 | custom fusion | bytes 33280 | tf_op jit(solution)/shard_map/scatter | solution.py:31
  26.9 6.3 %all-to-all-start = ((s32[4,1,2048]{2,1,0:T(1,128)}), s32[4,1,2048]{2,1,0:T(1,128)S(1)}, u32[]{:S(2)}, u32[]{:S(2)}) async-start(s32[4,1,2048]{2,1,0:T(1,128)} %bitcast.10), calls=%async_computation | async-start | bytes 65536 | tf_op jit(solution)/shard_map/all_to_all | solution.py:71
  33.2 12.4 %scatter_custom_fusion.1 = bf16[8192,128]{1,0:T(8,128)(2,1)} fusion(s32[4096]{0:T(1024)S(1)} %bitcast.139, bf16[1,4096,128]{2,1,0:T(8,128)(2,1)S(1)} %copy-done, bf16[]{:T(256)} %constant.30.clone.1), kind=kCustom, calls=%fused_computation.17 | custom fusion | bytes 3145730 | tf_op jit(solution)/shard_map/scatter | solution.py:30
  45.6 5.1 %all-to-all-start.1 = ((bf16[4,2048,128]{2,1,0:T(8,128)(2,1)}), bf16[4,2048,128]{2,1,0:T(8,128)(2,1)S(1)}, u32[]{:S(2)}, u32[]{:S(2)}) async-start(bf16[4,2048,128]{2,1,0:T(8,128)(2,1)} %bitcast.12), calls=%async_computation.1 | async-start | bytes 4194304 | tf_op jit(solution)/shard_map/all_to_all | solution.py:70
  50.8 47.6 %all-to-all-done.1 = bf16[4,2048,128]{2,1,0:T(8,128)(2,1)S(1)} async-done(((bf16[4,2048,128]{2,1,0:T(8,128)(2,1)}), bf16[4,2048,128]{2,1,0:T(8,128)(2,1)S(1)}, u32[]{:S(2)}, u32[]{:S(2)}) %all-to-all-start.1) | async-done | bytes 2097184 | tf_op jit(solution)/shard_map/all_to_all | solution.py:70
  98.4 56.3 %while.12 = (s32[]{:T(128)}, bf16[16,128,128]{2,1,0:T(8,128)(2,1)}, bf16[16,128]{1,0:T(8,128)(2,1)S(1)}, s32[16]{0:T(128)S(1)}, s32[4,2048]{1,0:T(4,128)S(1)}, /...) while((s32[]{:T(128)}, bf16[16,128,128]{2,1,0:T(8,128)(2,1)}, bf16[16,128]{1,0:T(8,128)(2,1)S(1)}, ...), condition=%wide.region_7.8_spmd, body=%wide.region_5.7_spmd.sunk | while | flops 272629760 | bytes 2296681 | solution.py:77
  99.7 1.5 fusion.68
  103.3 1.5 fusion.68
  106.8 1.5 fusion.68
  117.3 1.5 fusion.68
  120.9 1.5 fusion.68
  124.4 1.5 fusion.68
  131.4 1.5 fusion.68
  134.9 1.5 fusion.68
  138.5 1.5 fusion.68
  145.5 1.5 fusion.68
  152.5 1.5 fusion.68
  154.8 10.0 %psum.7 = bf16[2048]{0:T(1024)(128)(2,1)S(1)} all-reduce(bf16[2048]{0:T(1024)(128)(2,1)S(1)} %bitcast.141), channel_id=1, replica_groups=mesh['tile'=4,'chan'=4,'tm'=2] {'chan'}, use_global_device_ids=true, to_apply=%region_9.10 | all-reduce | flops 2048 | bytes 8192 | tf_op jit(solution)/shard_map/psum | solution.py:84
  164.9 24.3 %all-gather.3.cloned.1.call-done = bf16[4,2048,128]{2,1,0:T(8,128)(2,1)} async-done(((bf16[1,2048,128]{2,1,0:T(8,128)(2,1)}), bf16[4,2048,128]{2,1,0:T(8,128)(2,1)}) %all-gather.3.cloned.1.call-update) | async-done | bytes 2097168 | tf_op jit(solution)/shard_map/all_gather | solution.py:83
  189.2 2.2 reduce_sum.45
  193.4 8.1 %all-gather.5.cloned.1.call-done = bf16[32,64,256]{2,1,0:T(8,128)(2,1)} async-done(((bf16[32,64,128]{2,1,0:T(8,128)(2,1)}), bf16[32,64,256]{2,1,0:T(8,128)(2,1)}) %all-gather.5.cloned.1.call-update) | async-done | bytes 1048592 | tf_op jit(solution)/shard_map/all_gather | solution.py:90
  205.0 2.2 collective-permute-start
  208.5 2.9 %collective-permute-done.1 = bf16[2,32,64]{2,1,0:T(8,128)(2,1)S(1)} collective-permute-done((bf16[2,32,64]{2,1,0:T(8,128)(2,1)S(1)}, bf16[2,32,64]{2,1,0:T(8,128)(2,1)S(1)}, u32[]{:S(2)}, u32[]{:S(2)}) %collective-permute-start.1) | collective-permute-done | bytes 8224 | tf_op jit(solution)/shard_map/ppermute | solution.py:19
  212.3 11.0 %all_to_all.22 = bf16[4,2,2048]{2,1,0:T(2,128)(2,1)S(1)} all-to-all(bf16[4,2,2048]{2,1,0:T(2,128)(2,1)S(1)} %reshape.230), channel_id=1, replica_groups=mesh['tile'=4,'chan'=4,'tm'=2] {'tile'}, dimensions={0} | all-to-all | bytes 65536 | tf_op jit(solution)/shard_map/all_to_all | solution.py:111
  (134 shorter events, 52.2 us)
Async XLA Ops:
  6.5 26.7 %copy-start = (bf16[1,4096,128]{2,1,0:T(8,128)(2,1)S(1)}, bf16[1,4096,128]{2,1,0:T(8,128)(2,1)}, u32[]{:S(2)}) copy-start(bf16[1,4096,128]{2,1,0:T(8,128)(2,1)} %param.8) | copy-start | bytes 3145732
  26.9 18.8 %all-to-all-start = ((s32[4,1,2048]{2,1,0:T(1,128)}), s32[4,1,2048]{2,1,0:T(1,128)S(1)}, u32[]{:S(2)}, u32[]{:S(2)}) async-start(s32[4,1,2048]{2,1,0:T(1,128)} %bitcast.10), calls=%async_computation | async-start | bytes 65536 | tf_op jit(solution)/shard_map/all_to_all | solution.py:71
  45.6 52.7 %all-to-all-start.1 = ((bf16[4,2048,128]{2,1,0:T(8,128)(2,1)}), bf16[4,2048,128]{2,1,0:T(8,128)(2,1)S(1)}, u32[]{:S(2)}, u32[]{:S(2)}) async-start(bf16[4,2048,128]{2,1,0:T(8,128)(2,1)} %bitcast.12), calls=%async_computation.1 | async-start | bytes 4194304 | tf_op jit(solution)/shard_map/all_to_all | solution.py:70
  50.7 138.4 %all-gather.3.cloned.1.call-start = ((), (), s32[]{:S(2)}) async-start(), calls=%async_computation.3 | async-start | bytes 2621440 | tf_op jit(solution)/shard_map/all_gather | solution.py:83
  154.7 46.8 %all-gather.5.cloned.1.call-start = ((), (), s32[]{:S(2)}) async-start(), calls=%async_computation.4 | async-start | bytes 1572864 | tf_op jit(solution)/shard_map/all_gather | solution.py:90
  164.9 28.5 %copy-start.2 = (bf16[9,64]{1,0:T(8,128)(2,1)S(1)}, bf16[9,64]{1,0:T(8,128)(2,1)}, u32[]{:S(2)}) copy-start(bf16[9,64]{1,0:T(8,128)(2,1)} %param.12) | copy-start | bytes 3460
  191.3 12.7 %copy-start.1 = (bf16[4,256,64]{1,2,0:T(8,128)(2,1)S(1)}, bf16[4,256,64]{1,2,0:T(8,128)(2,1)}, u32[]{:S(2)}) copy-start(bf16[4,256,64]{1,2,0:T(8,128)(2,1)} %param.11) | copy-start | bytes 393220
  205.0 3.5 %collective-permute-start = (bf16[2,32,64]{2,1,0:T(8,128)(2,1)S(1)}, bf16[2,32,64]{2,1,0:T(8,128)(2,1)S(1)}, u32[]{:S(2)}, u32[]{:S(2)}) collective-permute-start(bf16[2,32,64]{2,1,0:T(8,128)(2,1)S(1)} %get-tuple-element.52), channel_id=1, source_target_pairs={{0,1},{1,8},{8,9},{9,16},{16,17},{17,24},{24,25},{2,3},{3,10},{10,... | collective-permute-start | bytes 24584 | tf_op jit(solution)/shard_map/ppermute | solution.py:18
  207.1 4.2 %collective-permute-start.1 = (bf16[2,32,64]{2,1,0:T(8,128)(2,1)S(1)}, bf16[2,32,64]{2,1,0:T(8,128)(2,1)S(1)}, u32[]{:S(2)}, u32[]{:S(2)}) collective-permute-start(bf16[2,32,64]{2,1,0:T(8,128)(2,1)S(1)} %get-tuple-element.53), channel_id=1, source_target_pairs={{1,0},{8,1},{9,8},{16,9},{17,16},{24,17},{25,24},{3,2},{10,3},{11,... | collective-permute-start | bytes 24584 | tf_op jit(solution)/shard_map/ppermute | solution.py:19
Sparse Core Ops, SparseCore 0:
  154.8 34.2 all-gather.2
  192.7 8.7 all-gather.4
